TPU v7x, 32 devices: a whole 2x2x4 slice. The times are simulated.
32 devices in a mesh: replica: 4 (over x, core), fsdp: 8 (over z, y).
Axes of the slice: x: 2, y: 2, z: 4, core: 2. Of those that a mesh axis runs over, the one named last changes fastest.
Arguments:
- byte_input: bfloat16 [32768, 768], P(('replica', 'fsdp')), may hold values from -6 to 6
- global_out: bfloat16 [32768, 768], P(('replica', 'fsdp')), may hold values from -6 to 6
- cotangent: bfloat16 [32768, 768], P(('replica', 'fsdp')), may hold values from -6 to 6
- seq_patches: int32 [4, 4], P('replica'), may hold values from 1 to 512, 1024 in all within a row
- last_fill: int32 [4, 4], P('replica'), may hold values from 1 to 8
- deal_slots: int32 [4, 1024], P('replica', 'fsdp'), may hold values from 0 to 1023, as said below
- first_gain: bfloat16 [768], P('fsdp'), may hold values from 0.5 to 1.5
- first_shift: bfloat16 [768], P('fsdp'), may hold values from -1.796875 to 1.796875
- qkv_weight: bfloat16 [768, 2304], P('fsdp'), may hold values from -0.21875 to 0.21875
- out_weight: bfloat16 [768, 768], P('fsdp'), may hold values from -0.4375 to 0.4375
- second_gain: bfloat16 [768], P('fsdp'), may hold values from 0.5 to 1.5
- second_shift: bfloat16 [768], P('fsdp'), may hold values from -1.796875 to 1.796875
- up_weight: bfloat16 [768, 3072], P('fsdp'), may hold values from -0.21875 to 0.21875
- up_bias: bfloat16 [3072], P('fsdp'), may hold values from -3 to 3
- down_weight: bfloat16 [3072, 768], P('fsdp'), may hold values from -0.15625 to 0.15625
- down_bias: bfloat16 [768], P('fsdp'), may hold values from -1.796875 to 1.796875
Outputs:
- layer_out: bfloat16 [32768, 768], P(('replica', 'fsdp'))
- grad_input: bfloat16 [32768, 768], P(('replica', 'fsdp'))
- grad_global: bfloat16 [32768, 768], P(('replica', 'fsdp'))
- grad_first_gain: float32 [768], P('fsdp')
- grad_first_shift: float32 [768], P('fsdp')
- grad_qkv_weight: float32 [768, 2304], P('fsdp')
- grad_out_weight: float32 [768, 768], P('fsdp')
- grad_second_gain: float32 [768], P('fsdp')
- grad_second_shift: float32 [768], P('fsdp')
- grad_up_weight: float32 [768, 3072], P('fsdp')
- grad_up_bias: float32 [3072], P('fsdp')
- grad_down_weight: float32 [3072, 768], P('fsdp')
- grad_down_bias: float32 [768], P('fsdp')
Inputs may be any that keep to these rules, and one draw needn't show every extreme that they name: `seq_patches`: row g gives the patches of the 4 sequences of group g in order; each row sums to 1024 and its largest entry is 512. `last_fill`: bytes used in the last patch of each sequence; the rest of that patch is padding. Each row is a permutation of 0 to 1023. Of the patches p in any aligned block of 128, exactly 16 have deal_slots in each aligned block of 128 positions.
All inputs are finite; a program needn't handle non-finite values.
Results may differ from a plain program's by a relative error of at most 0.017.
Values may be sent and summed in bfloat16 or wider, within the bound.
No kernel may reach another device: no remote copies, remote signals or barrier semaphores. Data moves between devices by JAX's collectives and lax.ppermute only.
A program may use at most 128 MiB of HBM per device.

v0:
```python
import jax
import jax.numpy as jnp
from jax import lax
from jax.sharding import PartitionSpec as P

HEADS = 12
HEAD_DIM = 64
PATCH = 8
EPSILON = 1e-05


def contract_rows(left, right):
    return lax.dot_general(
        left, right, (((0,), (0,)), ((), ())), preferred_element_type=jnp.float32
    )


def contract_cols(left, right):
    return lax.dot_general(
        left, right, (((1,), (1,)), ((), ())), preferred_element_type=jnp.float32
    )


def apply_layer_normalize(values, gain, shift):
    center = values - jnp.mean(values, axis=1, keepdims=True)
    inverse = lax.rsqrt(jnp.mean(jnp.square(center), axis=1, keepdims=True) + EPSILON)
    normed = center * inverse
    return (normed * gain + shift, normed, inverse)


def normalize_pullback(upstream, gain, normed, inverse):
    scaled = upstream * gain
    inner = (
        scaled
        - jnp.mean(scaled, axis=1, keepdims=True)
        - normed * jnp.mean(scaled * normed, axis=1, keepdims=True)
    )
    return (inverse * inner, jnp.sum(upstream * normed, axis=0), jnp.sum(upstream, axis=0))


def block_mask(span):
    index = jnp.arange(span, dtype=jnp.int32)
    return (index[:, None] // PATCH == index[None, :] // PATCH) & (index[None, :] <= index[:, None])


def attention_scores(queries, keys_part, allowed):
    raw = jnp.einsum(
        "gqhd,gkhd->ghqk", queries, keys_part, preferred_element_type=jnp.float32
    ) * HEAD_DIM ** (-0.5)
    return jnp.where(allowed, raw, -1e30)


def body(
    byte_input,
    global_out,
    cotangent,
    seq_patches,
    last_fill,
    deal_slots,
    first_gain,
    first_shift,
    qkv_weight,
    out_weight,
    second_gain,
    second_shift,
    up_weight,
    up_bias,
    down_weight,
    down_bias,
):
    row_count = byte_input.shape[0]
    model_width = byte_input.shape[1]
    patch_count = row_count // PATCH
    fsdp_count = lax.axis_size("fsdp")
    share = patch_count // fsdp_count
    patch_ids = lax.axis_index("fsdp") * patch_count + jnp.arange(patch_count, dtype=jnp.int32)
    seq_ends = jnp.cumsum(seq_patches[0])
    seq_ids = jnp.sum((patch_ids[:, None] >= seq_ends[None, :]).astype(jnp.int32), axis=1)
    seq_hits = (seq_ids[:, None] == jnp.arange(seq_ends.shape[0], dtype=jnp.int32)[None, :]).astype(
        jnp.int32
    )
    end_of = jnp.sum(seq_hits * seq_ends[None, :], axis=1)
    fill_of = jnp.sum(seq_hits * last_fill[0][None, :], axis=1)
    in_patch = jnp.arange(PATCH, dtype=jnp.int32)
    keep_byte = (
        (patch_ids != end_of - 1)[:, None] | (in_patch[None, :] < fill_of[:, None])
    ).reshape(row_count, 1)
    target = deal_slots[0] // patch_count
    dealt_slot = deal_slots[0] % patch_count
    dest_hits = (target[:, None] == jnp.arange(fsdp_count, dtype=jnp.int32)[None, :]).astype(
        jnp.int32
    )
    dest_rank = jnp.sum((jnp.cumsum(dest_hits, axis=0) - 1) * dest_hits, axis=1)
    send_place = target * share + dest_rank
    send_order = (
        jnp.zeros((patch_count,), jnp.int32)
        .at[send_place]
        .set(jnp.arange(patch_count, dtype=jnp.int32))
    )

    def pack_rows(values):
        return values.reshape(patch_count, PATCH, model_width)[send_order].reshape(
            row_count, model_width
        )

    def unpack_rows(values):
        return values.reshape(patch_count, PATCH, model_width)[send_place].reshape(
            row_count, model_width
        )

    arrived, arrived_slot = (
        lax.all_to_all(pack_rows(byte_input), "fsdp", split_axis=0, concat_axis=0, tiled=True),
        lax.all_to_all(dealt_slot[send_order], "fsdp", split_axis=0, concat_axis=0, tiled=True),
    )
    (
        gain_full,
        complete_shift_vector,
        qkv_full,
        outproj_full,
        gain_later,
        deferred_shift_vector,
        expand_full,
        expand_bias,
        reduce_full,
        reduce_bias,
    ) = (
        lax.all_gather(first_gain, "fsdp", axis=0, tiled=True),
        lax.all_gather(first_shift, "fsdp", axis=0, tiled=True),
        lax.all_gather(qkv_weight, "fsdp", axis=0, tiled=True),
        lax.all_gather(out_weight, "fsdp", axis=0, tiled=True),
        lax.all_gather(second_gain, "fsdp", axis=0, tiled=True),
        lax.all_gather(second_shift, "fsdp", axis=0, tiled=True),
        lax.all_gather(up_weight, "fsdp", axis=0, tiled=True),
        lax.all_gather(up_bias, "fsdp", axis=0, tiled=True),
        lax.all_gather(down_weight, "fsdp", axis=0, tiled=True),
        lax.all_gather(down_bias, "fsdp", axis=0, tiled=True),
    )
    attention_norm_gain = gain_full.astype(jnp.float32)
    feedforward_norm_gain = gain_later.astype(jnp.float32)
    global_rows = global_out.reshape(patch_count, PATCH, model_width)[arrived_slot].reshape(
        row_count, model_width
    )
    residual_input = arrived.astype(jnp.float32) + global_rows.astype(jnp.float32)
    attention_normed_input, attention_centered_scaled, attention_inverse_deviation = (
        apply_layer_normalize(
            residual_input, attention_norm_gain, complete_shift_vector.astype(jnp.float32)
        )
    )
    first_in = attention_normed_input.astype(jnp.bfloat16)
    qkv_rows = jnp.dot(first_in, qkv_full, preferred_element_type=jnp.float32).astype(jnp.bfloat16)
    blocks = row_count // 128

    def heads_of(values, start):
        return lax.slice_in_dim(values, start, start + model_width, axis=1).reshape(
            blocks, 128, HEADS, HEAD_DIM
        )

    queries = heads_of(qkv_rows, 0)
    keys_part = heads_of(qkv_rows, model_width)
    values_part = heads_of(qkv_rows, 2 * model_width)
    allowed = block_mask(128)
    scores = attention_scores(queries, keys_part, allowed)
    top_score = jnp.max(scores, axis=3, keepdims=True)
    expo = jnp.exp(scores - top_score)
    total = jnp.sum(expo, axis=3, keepdims=True)
    log_total = top_score + jnp.log(total)
    probs = (expo / total).astype(jnp.bfloat16)
    mixed = jnp.einsum("ghqk,gkhd->gqhd", probs, values_part, preferred_element_type=jnp.float32)
    attended = mixed.reshape(row_count, model_width).astype(jnp.bfloat16)
    residual_midway = residual_input + jnp.dot(
        attended, outproj_full, preferred_element_type=jnp.float32
    )
    feedforward_normed_input, feedforward_centered_scaled, feedforward_inverse_deviation = (
        apply_layer_normalize(
            residual_midway, feedforward_norm_gain, deferred_shift_vector.astype(jnp.float32)
        )
    )
    second_in = feedforward_normed_input.astype(jnp.bfloat16)
    pre_act = jnp.dot(
        second_in, expand_full, preferred_element_type=jnp.float32
    ) + expand_bias.astype(jnp.float32)
    activ = jax.nn.gelu(pre_act, approximate=False).astype(jnp.bfloat16)
    result = (
        residual_midway
        + jnp.dot(activ, reduce_full, preferred_element_type=jnp.float32)
        + reduce_bias.astype(jnp.float32)
    )
    returned = lax.all_to_all(
        result.astype(jnp.bfloat16), "fsdp", split_axis=0, concat_axis=0, tiled=True
    )
    layer_out = jnp.where(keep_byte, unpack_rows(returned), jnp.zeros((), jnp.bfloat16))
    masked_cot = jnp.where(keep_byte, cotangent, jnp.zeros((), jnp.bfloat16))
    upstream_b = lax.all_to_all(
        pack_rows(masked_cot), "fsdp", split_axis=0, concat_axis=0, tiled=True
    )
    upstream = upstream_b.astype(jnp.float32)
    grad_reduce_bias = jnp.sum(upstream, axis=0)
    grad_reduce = contract_rows(activ, upstream_b)
    grad_activ = contract_cols(upstream_b, reduce_full)
    density = jnp.exp(-0.5 * jnp.square(pre_act)) * 0.3989422804014327
    cumulative = 0.5 * (1.0 + jax.scipy.special.erf(pre_act * 0.7071067811865476))
    grad_pre = (grad_activ * (cumulative + pre_act * density)).astype(jnp.bfloat16)
    grad_expand_bias = jnp.sum(grad_pre.astype(jnp.float32), axis=0)
    grad_expand = contract_rows(second_in, grad_pre)
    gradient_feedforward_branch = contract_cols(grad_pre, expand_full)
    normalize_piece, gradient_feedforward_gain, gradient_feedforward_shift = normalize_pullback(
        gradient_feedforward_branch,
        feedforward_norm_gain,
        feedforward_centered_scaled,
        feedforward_inverse_deviation,
    )
    grad_middle = upstream + normalize_piece
    grad_branch = grad_middle.astype(jnp.bfloat16)
    grad_outproj = contract_rows(attended, grad_branch)
    grad_attended = (
        contract_cols(grad_branch, outproj_full)
        .astype(jnp.bfloat16)
        .reshape(blocks, 128, HEADS, HEAD_DIM)
    )
    scores_again = attention_scores(queries, keys_part, allowed)
    probs_again = jnp.exp(scores_again - log_total)
    grad_probs = jnp.einsum(
        "gqhd,gkhd->ghqk", grad_attended, values_part, preferred_element_type=jnp.float32
    )
    grad_values = jnp.einsum(
        "ghqk,gqhd->gkhd",
        probs_again.astype(jnp.bfloat16),
        grad_attended,
        preferred_element_type=jnp.float32,
    )
    grad_scores = (
        probs_again * (grad_probs - jnp.sum(probs_again * grad_probs, axis=3, keepdims=True))
    ).astype(jnp.bfloat16)
    grad_queries = jnp.einsum(
        "ghqk,gkhd->gqhd", grad_scores, keys_part, preferred_element_type=jnp.float32
    ) * HEAD_DIM ** (-0.5)
    grad_keys = jnp.einsum(
        "ghqk,gqhd->gkhd", grad_scores, queries, preferred_element_type=jnp.float32
    ) * HEAD_DIM ** (-0.5)
    grad_qkv = jnp.concatenate(
        [
            grad_queries.reshape(row_count, model_width),
            grad_keys.reshape(row_count, model_width),
            grad_values.reshape(row_count, model_width),
        ],
        axis=1,
    ).astype(jnp.bfloat16)
    grad_qkv_full = contract_rows(first_in, grad_qkv)
    gradient_attention_branch = contract_cols(grad_qkv, qkv_full)
    normalize_before_attention, gradient_attention_gain, gradient_attention_shift = (
        normalize_pullback(
            gradient_attention_branch,
            attention_norm_gain,
            attention_centered_scaled,
            attention_inverse_deviation,
        )
    )
    grad_base = (grad_middle + normalize_before_attention).astype(jnp.bfloat16)
    inverse_slot = (
        jnp.zeros((patch_count,), jnp.int32)
        .at[arrived_slot]
        .set(jnp.arange(patch_count, dtype=jnp.int32))
    )
    grad_global = grad_base.reshape(patch_count, PATCH, model_width)[inverse_slot].reshape(
        row_count, model_width
    )
    sent_back = lax.all_to_all(grad_base, "fsdp", split_axis=0, concat_axis=0, tiled=True)
    grad_input = unpack_rows(sent_back)
    owned = (
        lax.psum_scatter(
            gradient_attention_gain.astype(jnp.bfloat16), "fsdp", scatter_dimension=0, tiled=True
        ).astype(jnp.float32),
        lax.psum_scatter(
            gradient_attention_shift.astype(jnp.bfloat16), "fsdp", scatter_dimension=0, tiled=True
        ).astype(jnp.float32),
        lax.psum_scatter(
            grad_qkv_full.astype(jnp.bfloat16), "fsdp", scatter_dimension=0, tiled=True
        ).astype(jnp.float32),
        lax.psum_scatter(
            grad_outproj.astype(jnp.bfloat16), "fsdp", scatter_dimension=0, tiled=True
        ).astype(jnp.float32),
        lax.psum_scatter(
            gradient_feedforward_gain.astype(jnp.bfloat16), "fsdp", scatter_dimension=0, tiled=True
        ).astype(jnp.float32),
        lax.psum_scatter(
            gradient_feedforward_shift.astype(jnp.bfloat16), "fsdp", scatter_dimension=0, tiled=True
        ).astype(jnp.float32),
        lax.psum_scatter(
            grad_expand.astype(jnp.bfloat16), "fsdp", scatter_dimension=0, tiled=True
        ).astype(jnp.float32),
        lax.psum_scatter(
            grad_expand_bias.astype(jnp.bfloat16), "fsdp", scatter_dimension=0, tiled=True
        ).astype(jnp.float32),
        lax.psum_scatter(
            grad_reduce.astype(jnp.bfloat16), "fsdp", scatter_dimension=0, tiled=True
        ).astype(jnp.float32),
        lax.psum_scatter(
            grad_reduce_bias.astype(jnp.bfloat16), "fsdp", scatter_dimension=0, tiled=True
        ).astype(jnp.float32),
    )
    totals = (
        lax.psum(owned[0].astype(jnp.bfloat16), "replica").astype(jnp.float32),
        lax.psum(owned[1].astype(jnp.bfloat16), "replica").astype(jnp.float32),
        lax.psum(owned[2].astype(jnp.bfloat16), "replica").astype(jnp.float32),
        lax.psum(owned[3].astype(jnp.bfloat16), "replica").astype(jnp.float32),
        lax.psum(owned[4].astype(jnp.bfloat16), "replica").astype(jnp.float32),
        lax.psum(owned[5].astype(jnp.bfloat16), "replica").astype(jnp.float32),
        lax.psum(owned[6].astype(jnp.bfloat16), "replica").astype(jnp.float32),
        lax.psum(owned[7].astype(jnp.bfloat16), "replica").astype(jnp.float32),
        lax.psum(owned[8].astype(jnp.bfloat16), "replica").astype(jnp.float32),
        lax.psum(owned[9].astype(jnp.bfloat16), "replica").astype(jnp.float32),
    )
    return (
        layer_out,
        grad_input,
        grad_global,
        totals[0],
        totals[1],
        totals[2],
        totals[3],
        totals[4],
        totals[5],
        totals[6],
        totals[7],
        totals[8],
        totals[9],
    )


def solution(mesh):
    in_specs = (
        P(("replica", "fsdp"), None),
        P(("replica", "fsdp"), None),
        P(("replica", "fsdp"), None),
        P("replica", None),
        P("replica", None),
        P("replica", "fsdp"),
        P("fsdp"),
        P("fsdp"),
        P("fsdp", None),
        P("fsdp", None),
        P("fsdp"),
        P("fsdp"),
        P("fsdp", None),
        P("fsdp"),
        P("fsdp", None),
        P("fsdp"),
    )
    out_specs = (
        P(("replica", "fsdp"), None),
        P(("replica", "fsdp"), None),
        P(("replica", "fsdp"), None),
        P("fsdp"),
        P("fsdp"),
        P("fsdp", None),
        P("fsdp", None),
        P("fsdp"),
        P("fsdp"),
        P("fsdp", None),
        P("fsdp"),
        P("fsdp", None),
        P("fsdp"),
    )
    return jax.shard_map(body, mesh=mesh, in_specs=in_specs, out_specs=out_specs, check_vma=False)
```

profile of v0, /device:TPU:0, one launch (start us, length us, event | category | flops | bytes accessed | tf_op | source)
XLA Modules:
  0.0 805.4 jit_solution(18170484477021151799)
XLA Ops:
  14.1 7.3 all-to-all-start.1
  34.2 50.6 %all-reduce.12 = (bf16[768]{0:T(1024)(128)(2,1)S(1)}, bf16[768]{0:T(1024)(128)(2,1)S(1)}, bf16[768]{0:T(1024)(128)(2,1)S(1)}, bf16[768]{0:T(1024)(128)(2,1)S(1)}) all-reduce(bf16[768]{0:T(1024)(128)(2,1)S(1)} %dynamic-update-slice.1, bf16[768]{0:T(1024)(128)(2,1)S(1)} %dynamic-update-slice, ...), channel_id=1, replica_groups=mesh['replica'=4,'fsdp'=8] {'fsdp'}, use_global_device_ids=true, to_apply=%add.1 | all-reduce | flops 3072 | bytes 12288
  84.8 43.5 %all-gather = bf16[8,1,384]{2,1,0:T(2,128)(2,1)S(1)} all-gather(bf16[1,1,384]{2,1,0:T(2,128)(2,1)S(1)} %reshape.552), channel_id=1, replica_groups=mesh['replica'=4,'fsdp'=8] {'fsdp'}, dimensions={0}, use_global_device_ids=true | all-gather | bytes 6912 | tf_op jit(solution)/shard_map/all_gather | solution.py:134
  149.5 6.3 convolution_convert_fusion
  183.8 60.6 %all-gather.10.cloned.1.call-done = bf16[768,3072]{1,0:T(8,128)(2,1)} async-done(((bf16[96,3072]{1,0:T(8,128)(2,1)}), bf16[768,3072]{1,0:T(8,128)(2,1)}) %all-gather.10.cloned.1.call-update) | async-done | bytes 4718608 | tf_op jit(solution)/shard_map/all_gather | solution.py:133
  244.4 37.7 %fusion.2 = (bf16[1024,3072]{1,0:T(8,128)(2,1)}, f32[1024,3072]{1,0:T(8,128)}) fusion(f32[3072]{0:T(1024)S(1)} %bitcast.199, bf16[768,3072]{1,0:T(8,128)(2,1)} %all-gather.10.cloned.1.call-done, f32[1024,768]{1,0:T(8,128)} %copy-done.10, f32[768]{0:T(1024)S(1)} %convert_element_type.192, f32[768]{0:T(1024)S(1)} %convert_element_type.191, ...), kind=kOutput, calls=%fused_computation.12 | convolution fusion | flops 5043388416 | bytes 26765312 | tf_op jit(solution)/shard_map/dot_general | solution.py:179
  282.1 42.4 %all-gather.12.cloned.1.call-done = bf16[3072,768]{1,0:T(8,128)(2,1)} async-done(((bf16[384,768]{1,0:T(8,128)(2,1)}), bf16[3072,768]{1,0:T(8,128)(2,1)}) %all-gather.12.cloned.1.call-update) | async-done | bytes 4718608 | tf_op jit(solution)/shard_map/all_gather | solution.py:135
  324.5 12.5 %fusion.61 = (bf16[3072]{0:T(1024)(128)(2,1)S(1)}, bf16[1024,3072]{1,0:T(8,128)(2,1)S(1)}) fusion(f32[1024,3072]{1,0:T(8,128)} %get-tuple-element.60, f32[3072]{0:T(1024)S(1)} %bitcast.200, bf16[1024,768]{1,0:T(8,128)(2,1)} %bitcast.25, bf16[3072,768]{1,0:T(8,128)(2,1)} %all-gather.12.cloned.1.call-done), kind=kOutput, calls=%fused_computation.152 | convolution fusion | flops 4869583872 | bytes 25184256 | tf_op jit(solution)/shard_map/dot_general | solution.py:19
  337.1 5.7 multiply_reduce_fusion.1
  354.8 5.0 multiply_reduce_fusion
  367.2 4.8 fusion.28
  374.5 5.0 fusion.29
  384.2 5.5 convolution_convert_fusion.3
  390.1 10.4 %convolution_convert_fusion.2 = bf16[768,3072]{1,0:T(8,128)(2,1)} fusion(bf16[1024,3072]{1,0:T(8,128)(2,1)} %copy-done.43, f32[1024,768]{1,0:T(8,128)} %copy-done.10, f32[768]{0:T(1024)S(1)} %convert_element_type.192, f32[768]{0:T(1024)S(1)} %convert_element_type.191, f32[1024]{0:T(1024)S(1)} %add_rsqrt_fusion, f32[1024]{0:T(1024)S(1)} %broadcast_multiply_fusion.4), kind=kOutput, calls=%fused_computation.38 | convolution fusion | flops 4838129664 | bytes 14170112 | tf_op jit(solution)/shard_map/dot_general | solution.py:13
  400.6 9.1 %convolution_convert_fusion.1 = bf16[3072,768]{1,0:T(8,128)(2,1)} fusion(bf16[1024,3072]{1,0:T(8,128)(2,1)} %get-tuple-element.59, bf16[1024,768]{1,0:T(8,128)(2,1)} %bitcast.25), kind=kOutput, calls=%fused_computation.37 | convolution fusion | flops 4834197504 | bytes 12582912 | tf_op jit(solution)/shard_map/dot_general | solution.py:13
  412.5 9.6 %multiply_reduce_fusion.2 = (bf16[768]{0:T(1024)(128)(2,1)S(1)}, f32[1024]{0:T(1024)S(1)}, f32[1024]{0:T(1024)S(1)}, bf16[768]{0:T(1024)(128)(2,1)S(1)}, f32[1024,768]{1,0:T(8,128)}) fusion(f32[1024]{0:T(1024)S(1)} %copy-done.26, f32[1024]{0:T(1024)S(1)} %copy-done.22, bf16[128,8,768]{2,1,0:T(8,128)(2,1)S(1)} %copy-done.8, ...), kind=kOutput, calls=%fused_computation.45 | convolution fusion | flops 3633312256 | bytes 14571520 | tf_op jit(solution)/shard_map/dot_general | solution.py:19
  422.1 35.5 %all-reduce.11 = (bf16[768]{0:T(1024)(128)(2,1)S(1)}, bf16[768]{0:T(1024)(128)(2,1)S(1)}, bf16[768]{0:T(1024)(128)(2,1)S(1)}, bf16[768]{0:T(1024)(128)(2,1)S(1)}...) all-reduce(bf16[768]{0:T(1024)(128)(2,1)S(1)} %dynamic-update-slice, ...), channel_id=1, replica_groups=mesh['replica'=4,'fsdp'=8] {'fsdp'}, use_global_device_ids=true, to_apply=%add.4 | all-reduce | flops 7680 | bytes 30720
  457.7 9.9 %add_convert_fusion.1 = bf16[1024,768]{1,0:T(8,128)(2,1)} fusion(f32[1024,768]{1,0:T(8,128)} %copy-done.10, bf16[1024,3072]{1,0:T(8,128)(2,1)} %get-tuple-element.59, bf16[3072,768]{1,0:T(8,128)(2,1)} %all-gather.12.cloned.1.call-done, f32[768]{0:T(1024)S(1)} %convert_element_type.196), kind=kOutput, calls=%fused_computation.53 | convolution fusion | flops 4834197504 | bytes 15731712 | tf_op jit(solution)/shard_map/dot_general | solution.py:185
  476.4 28.1 %all-to-all-done.2 = bf16[8,128,768]{2,1,0:T(8,128)(2,1)} async-done(((bf16[8,128,768]{2,1,0:T(8,128)(2,1)}), bf16[8,128,768]{2,1,0:T(8,128)(2,1)}, u32[]{:S(2)}, u32[]{:S(2)}) %all-to-all-start.2) | async-done | bytes 1572896 | tf_op jit(solution)/shard_map/all_to_all | solution.py:188
  508.2 30.2 %reduce-scatter.5.cloned.1.call-done = bf16[96,2304]{1,0:T(8,128)(2,1)} async-done(((bf16[768,2304]{1,0:T(8,128)(2,1)}), bf16[96,2304]{1,0:T(8,128)(2,1)}) %reduce-scatter.5.cloned.1.call-update) | async-done | bytes 442384 | tf_op jit(solution)/shard_map/reduce_scatter | solution.py:276
  538.4 105.4 %reduce-scatter.9.cloned.1.call-done = bf16[96,3072]{1,0:T(8,128)(2,1)} async-done(((bf16[768,3072]{1,0:T(8,128)(2,1)}), bf16[96,3072]{1,0:T(8,128)(2,1)}) %reduce-scatter.9.cloned.1.call-update) | async-done | bytes 589840 | tf_op jit(solution)/shard_map/reduce_scatter | solution.py:288
  643.8 98.9 %reduce-scatter.11.cloned.1.call-done = bf16[384,768]{1,0:T(8,128)(2,1)} async-done(((bf16[3072,768]{1,0:T(8,128)(2,1)}), bf16[384,768]{1,0:T(8,128)(2,1)}) %reduce-scatter.11.cloned.1.call-update) | async-done | bytes 589840 | tf_op jit(solution)/shard_map/reduce_scatter | solution.py:294
  745.6 6.8 all-reduce.13
  765.3 26.4 %all-reduce.17.cloned.1.call-done = (bf16[96,2304]{1,0:T(8,128)(2,1)}, bf16[96,768]{1,0:T(8,128)(2,1)}, bf16[96,3072]{1,0:T(8,128)(2,1)}, bf16[384,768]{1,0:T(8,128)(2,1)}) async-done(((bf16[96,2304]{1,0:T(8,128)(2,1)}, bf16[96,768]{1,0:T(8,128)(2,1)}, bf16[96,3072]{1,0:T(8,128)(2,1)}, bf16[384,768]{1,0:T(8,128)(2,1)}), (bf16[96,2304]{1,0:T(8,128)(2,1)}, bf16[96,768]{1,0:T(8,128)(2,1)}, ...) | async-done | bytes 1769488 | tf_op jit(solution)/shard_map/psum | solution.py:304
  (234 shorter events, 131.2 us)
Async XLA Ops:
  7.2 14.2 %copy-start = (bf16[1024,768]{1,0:T(8,128)(2,1)S(1)}, bf16[1024,768]{1,0:T(8,128)(2,1)}, u32[]{:S(2)}) copy-start(bf16[1024,768]{1,0:T(8,128)(2,1)} %param.16) | copy-start | bytes 4718596
  7.2 142.3 %all-gather.6.cloned.1.call-start = ((), (), s32[]{:S(2)}) async-start(), calls=%async_computation.9 | async-start | bytes 3981312 | tf_op jit(solution)/shard_map/all_gather | solution.py:129
  7.9 169.8 %all-gather.8.cloned.1.call-start = ((), (), s32[]{:S(2)}) async-start(), calls=%async_computation.10 | async-start | bytes 1327104 | tf_op jit(solution)/shard_map/all_gather | solution.py:130
  8.7 235.7 %all-gather.10.cloned.1.call-start = ((), (), s32[]{:S(2)}) async-start(), calls=%async_computation.11 | async-start | bytes 5308416 | tf_op jit(solution)/shard_map/all_gather | solution.py:133
  14.1 13.7 %all-to-all-start.1 = ((s32[8,16,1]{1,2,0:T(1,128)}), s32[8,16,1]{1,2,0:T(1,128)S(1)}, u32[]{:S(2)}, u32[]{:S(2)}) async-start(s32[8,16,1]{1,2,0:T(1,128)} %bitcast.11), calls=%async_computation.1 | async-start | bytes 8192 | tf_op jit(solution)/shard_map/all_to_all | solution.py:113
  21.5 63.3 %copy-start.30 = (bf16[384]{0:T(512)(128)(2,1)S(1)}, bf16[384]{0:T(512)(128)(2,1)}, u32[]{:S(2)}) copy-start(bf16[384]{0:T(512)(128)(2,1)} %param.29) | copy-start | bytes 2308
  21.5 106.8 %copy-start.41 = (s32[1,4]{1,0:T(1,128)S(1)}, s32[1,4]{1,0:T(1,128)}, u32[]{:S(2)}) copy-start(s32[1,4]{1,0:T(1,128)} %param.19) | copy-start | bytes 52
  21.5 107.1 %copy-start.31 = (s32[1,4]{1,0:T(1,128)S(1)}, s32[1,4]{1,0:T(1,128)}, u32[]{:S(2)}) copy-start(s32[1,4]{1,0:T(1,128)} %param.20) | copy-start | bytes 52
  27.8 110.2 %all-to-all-start = ((bf16[8,128,768]{2,1,0:T(8,128)(2,1)}), bf16[8,128,768]{2,1,0:T(8,128)(2,1)S(1)}, u32[]{:S(2)}, u32[]{:S(2)}) async-start(bf16[8,128,768]{2,1,0:T(8,128)(2,1)} %bitcast.8), calls=%async_computation | async-start | bytes 3145728 | tf_op jit(solution)/shard_map/all_to_all | solution.py:112
  31.4 293.1 %all-gather.12.cloned.1.call-start = ((), (), s32[]{:S(2)}) async-start(), calls=%async_computation.12 | async-start | bytes 5308416 | tf_op jit(solution)/shard_map/all_gather | solution.py:135
  84.8 61.1 %copy-start.23 = (f32[768]{0:T(1024)}, f32[768]{0:T(1024)S(1)}, u32[]{:S(2)}) copy-start(f32[768]{0:T(1024)S(1)} %convert_element_type.183) | copy-start | bytes 9220
  138.0 144.1 %all-to-all-start.3 = ((bf16[8,128,768]{2,1,0:T(8,128)(2,1)}), bf16[8,128,768]{2,1,0:T(8,128)(2,1)}, u32[]{:S(2)}, u32[]{:S(2)}) async-start(bf16[8,128,768]{2,1,0:T(8,128)(2,1)} %bitcast.186), calls=%async_computation.3 | async-start | bytes 3145728 | tf_op jit(solution)/shard_map/all_to_all | solution.py:193
  142.3 365.8 %reduce-scatter.7.cloned.1.call-start = ((), (), s32[]{:S(2)}) async-start(), calls=%async_computation.14 | async-start | bytes 1327104 | tf_op jit(solution)/shard_map/reduce_scatter | solution.py:279
  324.5 12.5 %copy-start.11 = (f32[1024,768]{1,0:T(8,128)S(1)}, f32[1024,768]{1,0:T(8,128)}, u32[]{:S(2)}) copy-start(f32[1024,768]{1,0:T(8,128)} %copy-done.10) | copy-start | bytes 9437188
  324.5 12.6 %copy-start.35 = (bf16[768,3072]{1,0:T(8,128)(2,1)S(1)}, bf16[768,3072]{1,0:T(8,128)(2,1)}, u32[]{:S(2)}) copy-start(bf16[768,3072]{1,0:T(8,128)(2,1)} %all-gather.10.cloned.1.call-done) | copy-start | bytes 14155780
  367.0 171.4 %reduce-scatter.5.cloned.1.call-start = ((), (), s32[]{:S(2)}) async-start(), calls=%async_computation.13 | async-start | bytes 3981312 | tf_op jit(solution)/shard_map/reduce_scatter | solution.py:276
  389.7 254.1 %reduce-scatter.9.cloned.1.call-start = ((), (), s32[]{:S(2)}) async-start(), calls=%async_computation.15 | async-start | bytes 5308416 | tf_op jit(solution)/shard_map/reduce_scatter | solution.py:288
  400.6 342.1 %reduce-scatter.11.cloned.1.call-start = ((), (), s32[]{:S(2)}) async-start(), calls=%async_computation.16 | async-start | bytes 5308416 | tf_op jit(solution)/shard_map/reduce_scatter | solution.py:294
  467.6 36.8 %all-to-all-start.2 = ((bf16[8,128,768]{2,1,0:T(8,128)(2,1)}), bf16[8,128,768]{2,1,0:T(8,128)(2,1)}, u32[]{:S(2)}, u32[]{:S(2)}) async-start(bf16[8,128,768]{2,1,0:T(8,128)(2,1)} %bitcast.195), calls=%async_computation.2 | async-start | bytes 3145728 | tf_op jit(solution)/shard_map/all_to_all | solution.py:188
  476.3 267.6 %copy-start.33 = (s32[128]{0:T(128)S(1)}, s32[128]{0:T(128)}, u32[]{:S(2)}) copy-start(s32[128]{0:T(128)} %copy-done.32) | copy-start | bytes 1540
  476.3 279.2 %copy-start.9 = (bf16[1024,768]{1,0:T(8,128)(2,1)S(1)}, bf16[1024,768]{1,0:T(8,128)(2,1)}, u32[]{:S(2)}) copy-start(bf16[1024,768]{1,0:T(8,128)(2,1)} %add_convert_fusion) | copy-start | bytes 4718596
  504.4 256.2 %all-to-all-start.4 = ((bf16[8,128,768]{2,1,0:T(8,128)(2,1)}), bf16[8,128,768]{2,1,0:T(8,128)(2,1)S(1)}, u32[]{:S(2)}, u32[]{:S(2)}) async-start(bf16[8,128,768]{2,1,0:T(8,128)(2,1)} %bitcast.174), calls=%async_computation.4 | async-start | bytes 3145728 | tf_op jit(solution)/shard_map/all_to_all | solution.py:267
  508.1 283.6 %all-reduce.17.cloned.1.call-start = ((), (), s32[]{:S(2)}) async-start(), calls=%async_computation.17 | async-start | bytes 3538944 | tf_op jit(solution)/shard_map/psum | solution.py:304
  762.4 36.2 %copy-start.1 = (bf16[1024,768]{1,0:T(8,128)(2,1)S(1)}, bf16[1024,768]{1,0:T(8,128)(2,1)}, u32[]{:S(2)}) copy-start(bf16[1024,768]{1,0:T(8,128)(2,1)} %param.16) | copy-start | bytes 4718596
  (36 other events, 162.9 us)
Sparse Core Ops, SparseCore 0:
  10.2 92.3 all-gather.5
  104.8 45.2 all-gather.7
  152.3 92.0 all-gather.9
  246.4 78.0 all-gather.11
  367.1 62.1 reduce-scatter.6
  432.8 105.5 reduce-scatter.4
  542.0 101.7 reduce-scatter.8
  647.4 95.2 reduce-scatter.10
  745.3 46.3 all-reduce.16
where the time goes:
time: 813 us; the launch traced here: 805 us
  waiting for transfers between devices  399 us (49%)
  matrix products  137 us (17%)
  blocking collectives  136 us (17%)
  local copies, waits for them, and re-layouts  52.6 us (6%)
  other arithmetic  38.7 us (5%)
  starting transfers between devices  24.1 us (3%)
  between operations  16.9 us (2%)
    reduce_scatter x1, waiting for transfers between devices, body(): lax.psum_scatter(grad_expand.astype(jnp.bfloat16), 'fsdp', scatter_dimens...  105 us
    reduce_scatter x1, waiting for transfers between devices, body(): lax.psum_scatter(grad_reduce.astype(jnp.bfloat16), 'fsdp', scatter_dimens...  98.9 us
    unnamed x2, blocking collectives  86.1 us
    all_gather x1, waiting for transfers between devices, body(): lax.all_gather(up_weight, 'fsdp', axis=0, tiled=True)  60.6 us
    all_gather x1, blocking collectives, body(): lax.all_gather(up_bias, 'fsdp', axis=0, tiled=True)  43.5 us
    all_gather x1, waiting for transfers between devices, body(): lax.all_gather(down_weight, 'fsdp', axis=0, tiled=True)  42.4 us
    dot_general x1, matrix products, body(): jnp.dot(second_in, expand_full, preferred_element_type=jnp.float32)  37.7 us
    dot_general x4, matrix products, contract_cols(): lax.dot_general(left, right, (((1,), (1,)), ((), ())), preferred_element_...  31.2 us
  transfers between devices with their start and end apart: 14, of which 8 were waited for; matrix products, arithmetic and copies ran while one was open for 21% of the time, Pallas kernels for 0%

commit v1 on v0

--- a/solution.py
+++ b/solution.py
@@ -7,6 +7,19 @@
 HEAD_DIM = 64
 PATCH = 8
 EPSILON = 1e-05
+
+
+def collect(x, axis, dim):
+    ways = lax.axis_size(axis)
+    up = [(d, (d + 1) % ways) for d in range(ways)]
+    down = [(d, (d - 1) % ways) for d in range(ways)]
+    earlier, later = ([x], [x])
+    for _ in range(ways // 2):
+        earlier.append(lax.ppermute(earlier[-1], axis, up))
+    for _ in range((ways - 1) // 2):
+        later.append(lax.ppermute(later[-1], axis, down))
+    line = jnp.concatenate([*earlier[::-1], *later[1:]], axis=dim)
+    return jnp.roll(line, (lax.axis_index(axis) - ways // 2) * x.shape[dim], axis=dim)
 
 
 def contract_rows(left, right):
@@ -132,7 +145,7 @@
         lax.all_gather(second_shift, "fsdp", axis=0, tiled=True),
         lax.all_gather(up_weight, "fsdp", axis=0, tiled=True),
         lax.all_gather(up_bias, "fsdp", axis=0, tiled=True),
-        lax.all_gather(down_weight, "fsdp", axis=0, tiled=True),
+        collect(down_weight, "fsdp", 0),
         lax.all_gather(down_bias, "fsdp", axis=0, tiled=True),
     )
     attention_norm_gain = gain_full.astype(jnp.float32)

time: 813 us -> 826 us (1.016)
  waiting for transfers between devices: 399 us -> 354 us
  starting transfers between devices: 24.1 us -> 46.9 us
  local copies, waits for them, and re-layouts: 52.6 us -> 73.9 us
  blocking collectives: 136 us -> 150 us
    ppermute x0 -> x7, waiting for transfers between devices: none -> 66.1 us  [the longest x4 65 us: collect(): earlier.append(lax.ppermute(earlier[-1], axis, up))]
    all_gather x1 -> x0, waiting for transfers between devices: 42.4 us -> none  [body(): lax.all_gather(down_weight, 'fsdp', axis=0, tiled=True)]
    all_gather x1, waiting for transfers between devices: 60.6 us -> 26.9 us  [body(): lax.all_gather(up_weight, 'fsdp', axis=0, tiled=True)]
    unnamed x2, blocking collectives: 86.1 us -> 115 us
    all_to_all x1, waiting for transfers between devices: 28.1 us -> 0.01 us  [body(): lax.all_to_all(result.astype(jnp.bfloat16), 'fsdp', split_axis=0, concat_...]
    unnamed x116 -> x131, local copies, waits for them, and re-layouts: 22.7 us -> 44.1 us
    ppermute x0 -> x7, starting transfers between devices: none -> 19.3 us  [the longest x3 11.1 us: collect(): later.append(lax.ppermute(later[-1], axis, down))]
    all_gather x1, blocking collectives: 43.5 us -> 28.1 us  [body(): lax.all_gather(up_bias, 'fsdp', axis=0, tiled=True)]
  transfers between devices with their start and end apart: 14 -> 20, of which waited for: 8 -> 9; matrix products, arithmetic and copies ran while one was open for 21% -> 23% of each run, Pallas kernels for 0% -> 0%
where the time goes in v1:
time: 826 us; the launch traced here: 817 us
  waiting for transfers between devices  354 us (43%)
  blocking collectives  150 us (18%)
  matrix products  134 us (16%)
  local copies, waits for them, and re-layouts  73.9 us (9%)
  starting transfers between devices  46.9 us (6%)
  other arithmetic  40.6 us (5%)
  between operations  17.2 us (2%)
    unnamed x2, blocking collectives  115 us
    reduce_scatter x1, waiting for transfers between devices, body(): lax.psum_scatter(grad_expand.astype(jnp.bfloat16), 'fsdp', scatter_dimens...  102 us
    reduce_scatter x1, waiting for transfers between devices, body(): lax.psum_scatter(grad_reduce.astype(jnp.bfloat16), 'fsdp', scatter_dimens...  98.8 us
    ppermute x4, waiting for transfers between devices, collect(): earlier.append(lax.ppermute(earlier[-1], axis, up))  65 us
    unnamed x131, local copies, waits for them, and re-layouts  44.1 us
    dot_general x1, matrix products, body(): jnp.dot(second_in, expand_full, preferred_element_type=jnp.float32)  37.3 us
    dot_general x4, matrix products, contract_cols(): lax.dot_general(left, right, (((1,), (1,)), ((), ())), preferred_element_...  30.3 us
    psum x1, waiting for transfers between devices, body(): lax.psum(owned[2].astype(jnp.bfloat16), 'replica').astype(jnp.float32)  29.4 us
  transfers between devices with their start and end apart: 20, of which 9 were waited for; matrix products, arithmetic and copies ran while one was open for 23% of the time, Pallas kernels for 0%

profile of v1, /device:TPU:0, one launch (start us, length us, event | category | flops | bytes accessed | tf_op | source)
XLA Modules:
  0.0 816.8 jit_solution(1610542844917491267)
XLA Ops:
  17.6 24.4 %collective-permute-done = bf16[384,768]{1,0:T(8,128)(2,1)S(1)} collective-permute-done((bf16[384,768]{1,0:T(8,128)(2,1)}, bf16[384,768]{1,0:T(8,128)(2,1)S(1)}, u32[]{:S(2)}, u32[]{:S(2)}) %collective-permute-start) | collective-permute-done | bytes 589856 | tf_op jit(solution)/shard_map/ppermute | solution.py:18
  53.6 11.9 %collective-permute-done.1 = bf16[384,768]{1,0:T(8,128)(2,1)} collective-permute-done((bf16[384,768]{1,0:T(8,128)(2,1)S(1)}, bf16[384,768]{1,0:T(8,128)(2,1)}, u32[]{:S(2)}, u32[]{:S(2)}) %collective-permute-start.1) | collective-permute-done | bytes 589856 | tf_op jit(solution)/shard_map/ppermute | solution.py:18
  67.6 6.1 all-to-all-start
  80.1 28.7 %collective-permute-done.2 = bf16[384,768]{1,0:T(8,128)(2,1)} collective-permute-done((bf16[384,768]{1,0:T(8,128)(2,1)}, bf16[384,768]{1,0:T(8,128)(2,1)}, u32[]{:S(2)}, u32[]{:S(2)}) %collective-permute-start.2) | collective-permute-done | bytes 589856 | tf_op jit(solution)/shard_map/ppermute | solution.py:18
  113.8 37.6 %all-reduce.12 = (bf16[768]{0:T(1024)(128)(2,1)S(1)}, bf16[768]{0:T(1024)(128)(2,1)S(1)}, bf16[768]{0:T(1024)(128)(2,1)S(1)}, bf16[768]{0:T(1024)(128)(2,1)S(1)}) all-reduce(bf16[768]{0:T(1024)(128)(2,1)S(1)} %dynamic-update-slice.1, bf16[768]{0:T(1024)(128)(2,1)S(1)} %dynamic-update-slice, ...), channel_id=1, replica_groups=mesh['replica'=4,'fsdp'=8] {'fsdp'}, use_global_device_ids=true, to_apply=%add.1 | all-reduce | flops 3072 | bytes 12288
  151.6 28.1 %all-gather = bf16[8,1,384]{2,1,0:T(2,128)(2,1)S(1)} all-gather(bf16[1,1,384]{2,1,0:T(2,128)(2,1)S(1)} %reshape.552), channel_id=1, replica_groups=mesh['replica'=4,'fsdp'=8] {'fsdp'}, dimensions={0}, use_global_device_ids=true | all-gather | bytes 6912 | tf_op jit(solution)/shard_map/all_gather | solution.py:147
  215.8 6.4 all-to-all-start.3
  229.4 6.3 convolution_convert_fusion
  262.9 26.9 %all-gather.9.cloned.1.call-done = bf16[768,3072]{1,0:T(8,128)(2,1)} async-done(((bf16[96,3072]{1,0:T(8,128)(2,1)}), bf16[768,3072]{1,0:T(8,128)(2,1)}) %all-gather.9.cloned.1.call-update) | async-done | bytes 4718608 | tf_op jit(solution)/shard_map/all_gather | solution.py:146
  289.8 37.3 %fusion.2 = (bf16[1024,3072]{1,0:T(8,128)(2,1)}, f32[1024,3072]{1,0:T(8,128)}) fusion(f32[3072]{0:T(1024)S(1)} %bitcast.197, bf16[768,3072]{1,0:T(8,128)(2,1)} %all-gather.9.cloned.1.call-done, f32[1024,768]{1,0:T(8,128)} %copy-done.9, f32[768]{0:T(1024)S(1)} %convert_element_type.192, f32[768]{0:T(1024)S(1)} %convert_element_type.191, ...), kind=kOutput, calls=%fused_computation.12 | convolution fusion | flops 5043388416 | bytes 26765312 | tf_op jit(solution)/shard_map/dot_general | solution.py:192
  327.1 13.0 %fusion.68 = (bf16[3072]{0:T(1024)(128)(2,1)S(1)}, bf16[1024,3072]{1,0:T(8,128)(2,1)S(1)}) fusion(f32[1024,3072]{1,0:T(8,128)} %get-tuple-element.60, f32[3072]{0:T(1024)S(1)} %bitcast.198, bf16[1024,768]{1,0:T(8,128)(2,1)} %bitcast.25, bf16[6144,768]{1,0:T(8,128)(2,1)} %constant_dynamic-update-slice_fusion, s32[]{:T(128)S(6)} %select_n.106), kind=kOutput, calls=%fused_computation.173 | convolution fusion | flops 4869583872 | bytes 25184260 | tf_op jit(solution)/shard_map/dot_general | solution.py:32
  340.1 5.7 multiply_reduce_fusion.1
  362.0 7.2 multiply_reduce_fusion
  370.9 6.5 multiply_convert_fusion.1
  392.3 10.5 %convolution_convert_fusion.2 = bf16[768,3072]{1,0:T(8,128)(2,1)} fusion(bf16[1024,3072]{1,0:T(8,128)(2,1)} %copy-done.45, f32[1024,768]{1,0:T(8,128)} %copy-done.9, f32[768]{0:T(1024)S(1)} %convert_element_type.192, f32[768]{0:T(1024)S(1)} %convert_element_type.191, f32[1024]{0:T(1024)S(1)} %add_rsqrt_fusion, f32[1024]{0:T(1024)S(1)} %broadcast_multiply_fusion.4), kind=kOutput, calls=%fused_computation.38 | convolution fusion | flops 4838129664 | bytes 14170112 | tf_op jit(solution)/shard_map/dot_general | solution.py:26
  402.9 9.2 %convolution_convert_fusion.1 = bf16[3072,768]{1,0:T(8,128)(2,1)} fusion(bf16[1024,3072]{1,0:T(8,128)(2,1)} %get-tuple-element.59, bf16[1024,768]{1,0:T(8,128)(2,1)} %bitcast.25), kind=kOutput, calls=%fused_computation.37 | convolution fusion | flops 4834197504 | bytes 12582912 | tf_op jit(solution)/shard_map/dot_general | solution.py:26
  414.0 8.3 %multiply_reduce_fusion.2 = (bf16[768]{0:T(1024)(128)(2,1)S(1)}, f32[1024]{0:T(1024)S(1)}, f32[1024]{0:T(1024)S(1)}, bf16[768]{0:T(1024)(128)(2,1)S(1)}, f32[1024,768]{1,0:T(8,128)S(1)}) fusion(f32[1024]{0:T(1024)S(1)} %copy-done.30, f32[1024]{0:T(1024)S(1)} %copy-done.26, bf16[128,8,768]{2,1,0:T(8,128)(2,1)S(1)} %copy-done.7, ...), kind=kOutput, calls=%fused_computation.48 | convolution fusion | flops 3633312256 | bytes 14571520 | tf_op jit(solution)/shard_map/dot_general | solution.py:32
  431.5 77.8 %all-reduce.11 = (bf16[768]{0:T(1024)(128)(2,1)S(1)}, bf16[768]{0:T(1024)(128)(2,1)S(1)}, bf16[768]{0:T(1024)(128)(2,1)S(1)}, bf16[768]{0:T(1024)(128)(2,1)S(1)}...) all-reduce(bf16[768]{0:T(1024)(128)(2,1)S(1)} %dynamic-update-slice, ...), channel_id=1, replica_groups=mesh['replica'=4,'fsdp'=8] {'fsdp'}, use_global_device_ids=true, to_apply=%add.4 | all-reduce | flops 7680 | bytes 30720
  509.3 10.0 %add_convert_fusion.1 = bf16[1024,768]{1,0:T(8,128)(2,1)} fusion(f32[1024,768]{1,0:T(8,128)} %copy-done.9, bf16[1024,3072]{1,0:T(8,128)(2,1)} %get-tuple-element.59, bf16[6144,768]{1,0:T(8,128)(2,1)} %constant_dynamic-update-slice_fusion, s32[]{:T(128)S(6)} %select_n.106, f32[768]{0:T(1024)S(1)} %convert_element_type.196), kind=kOutput, calls=%fused_computation.56 | convolution fusion | flops 4834197504 | bytes 15731716 | tf_op jit(solution)/shard_map/dot_general | solution.py:198
  523.9 28.6 %reduce-scatter.5.cloned.1.call-done = bf16[96,2304]{1,0:T(8,128)(2,1)} async-done(((bf16[768,2304]{1,0:T(8,128)(2,1)}), bf16[96,2304]{1,0:T(8,128)(2,1)}) %reduce-scatter.5.cloned.1.call-update) | async-done | bytes 442384 | tf_op jit(solution)/shard_map/reduce_scatter | solution.py:289
  552.6 102.3 %reduce-scatter.9.cloned.1.call-done = bf16[96,3072]{1,0:T(8,128)(2,1)} async-done(((bf16[768,3072]{1,0:T(8,128)(2,1)}), bf16[96,3072]{1,0:T(8,128)(2,1)}) %reduce-scatter.9.cloned.1.call-update) | async-done | bytes 589840 | tf_op jit(solution)/shard_map/reduce_scatter | solution.py:301
  654.9 98.8 %reduce-scatter.11.cloned.1.call-done = bf16[384,768]{1,0:T(8,128)(2,1)} async-done(((bf16[3072,768]{1,0:T(8,128)(2,1)}), bf16[384,768]{1,0:T(8,128)(2,1)}) %reduce-scatter.11.cloned.1.call-update) | async-done | bytes 589840 | tf_op jit(solution)/shard_map/reduce_scatter | solution.py:307
  756.7 6.5 all-reduce.13
  773.4 29.4 %all-reduce.17.cloned.1.call-done = (bf16[96,2304]{1,0:T(8,128)(2,1)}, bf16[96,768]{1,0:T(8,128)(2,1)}, bf16[96,3072]{1,0:T(8,128)(2,1)}, bf16[384,768]{1,0:T(8,128)(2,1)}) async-done(((bf16[96,2304]{1,0:T(8,128)(2,1)}, bf16[96,768]{1,0:T(8,128)(2,1)}, bf16[96,3072]{1,0:T(8,128)(2,1)}, bf16[384,768]{1,0:T(8,128)(2,1)}), (bf16[96,2304]{1,0:T(8,128)(2,1)}, bf16[96,768]{1,0:T(8,128)(2,1)}, ...) | async-done | bytes 1769488 | tf_op jit(solution)/shard_map/psum | solution.py:317
  (260 shorter events, 171.8 us)
Async XLA Ops:
  7.2 58.5 %copy-start = (bf16[1024,768]{1,0:T(8,128)(2,1)S(1)}, bf16[1024,768]{1,0:T(8,128)(2,1)}, u32[]{:S(2)}) copy-start(bf16[1024,768]{1,0:T(8,128)(2,1)} %param.16) | copy-start | bytes 4718596
  7.2 222.2 %all-gather.5.cloned.1.call-start = ((), (), s32[]{:S(2)}) async-start(), calls=%async_computation.9 | async-start | bytes 3981312 | tf_op jit(solution)/shard_map/all_gather | solution.py:142
  7.9 248.8 %all-gather.7.cloned.1.call-start = ((), (), s32[]{:S(2)}) async-start(), calls=%async_computation.10 | async-start | bytes 1327104 | tf_op jit(solution)/shard_map/all_gather | solution.py:143
  8.7 33.3 %collective-permute-start = (bf16[384,768]{1,0:T(8,128)(2,1)}, bf16[384,768]{1,0:T(8,128)(2,1)S(1)}, u32[]{:S(2)}, u32[]{:S(2)}) collective-permute-start(bf16[384,768]{1,0:T(8,128)(2,1)} %param.30), channel_id=1, source_target_pairs={{0,1},{1,2},{2,3},{3,4},{4,5},{5,6},{6,7},{7,0},{8,9},{9,10},{10,1... | collective-permute-start | bytes 1769480 | tf_op jit(solution)/shard_map/ppermute | solution.py:18
  11.7 63.6 %collective-permute-start.4 = (bf16[384,768]{1,0:T(8,128)(2,1)}, bf16[384,768]{1,0:T(8,128)(2,1)}, u32[]{:S(2)}, u32[]{:S(2)}) collective-permute-start(bf16[384,768]{1,0:T(8,128)(2,1)} %param.30), channel_id=1, source_target_pairs={{0,7},{1,0},{2,1},{3,2},{4,3},{5,4},{6,5},{7,6},{8,15},{9,8},{10,9... | collective-permute-start | bytes 1769480 | tf_op jit(solution)/shard_map/ppermute | solution.py:20
  42.0 23.5 %collective-permute-start.1 = (bf16[384,768]{1,0:T(8,128)(2,1)S(1)}, bf16[384,768]{1,0:T(8,128)(2,1)}, u32[]{:S(2)}, u32[]{:S(2)}) collective-permute-start(bf16[384,768]{1,0:T(8,128)(2,1)S(1)} %collective-permute-done), channel_id=1, source_target_pairs={{0,1},{1,2},{2,3},{3,4},{4,5},{5,6},{6,7},{7,0},{8,9},{9,10},{10,1... | collective-permute-start | bytes 1769480 | tf_op jit(solution)/shard_map/ppermute | solution.py:18
  46.3 21.2 %all-to-all-start.1 = ((s32[8,16,1]{1,2,0:T(1,128)}), s32[8,16,1]{1,2,0:T(1,128)S(1)}, u32[]{:S(2)}, u32[]{:S(2)}) async-start(s32[8,16,1]{1,2,0:T(1,128)} %bitcast.11), calls=%async_computation.1 | async-start | bytes 8192 | tf_op jit(solution)/shard_map/all_to_all | solution.py:126
  51.2 238.6 %all-gather.9.cloned.1.call-start = ((), (), s32[]{:S(2)}) async-start(), calls=%async_computation.11 | async-start | bytes 5308416 | tf_op jit(solution)/shard_map/all_gather | solution.py:146
  65.5 43.3 %collective-permute-start.2 = (bf16[384,768]{1,0:T(8,128)(2,1)}, bf16[384,768]{1,0:T(8,128)(2,1)}, u32[]{:S(2)}, u32[]{:S(2)}) collective-permute-start(bf16[384,768]{1,0:T(8,128)(2,1)} %collective-permute-done.1), channel_id=1, source_target_pairs={{0,1},{1,2},{2,3},{3,4},{4,5},{5,6},{6,7},{7,0},{8,9},{9,10},{10,1... | collective-permute-start | bytes 1769480 | tf_op jit(solution)/shard_map/ppermute | solution.py:18
  67.6 148.3 %all-to-all-start = ((bf16[8,128,768]{2,1,0:T(8,128)(2,1)}), bf16[8,128,768]{2,1,0:T(8,128)(2,1)S(1)}, u32[]{:S(2)}, u32[]{:S(2)}) async-start(bf16[8,128,768]{2,1,0:T(8,128)(2,1)} %bitcast.8), calls=%async_computation | async-start | bytes 3145728 | tf_op jit(solution)/shard_map/all_to_all | solution.py:125
  75.4 111.5 %collective-permute-start.5 = (bf16[384,768]{1,0:T(8,128)(2,1)}, bf16[384,768]{1,0:T(8,128)(2,1)}, u32[]{:S(2)}, u32[]{:S(2)}) collective-permute-start(bf16[384,768]{1,0:T(8,128)(2,1)} %collective-permute-done.4), channel_id=1, source_target_pairs={{0,7},{1,0},{2,1},{3,2},{4,3},{5,4},{6,5},{7,6},{8,15},{9,8},{10,9... | collective-permute-start | bytes 1769480 | tf_op jit(solution)/shard_map/ppermute | solution.py:20
  108.8 81.4 %collective-permute-start.3 = (bf16[384,768]{1,0:T(8,128)(2,1)}, bf16[384,768]{1,0:T(8,128)(2,1)}, u32[]{:S(2)}, u32[]{:S(2)}) collective-permute-start(bf16[384,768]{1,0:T(8,128)(2,1)} %collective-permute-done.2), channel_id=1, source_target_pairs={{0,1},{1,2},{2,3},{3,4},{4,5},{5,6},{6,7},{7,0},{8,9},{9,10},{10,1... | collective-permute-start | bytes 1769480 | tf_op jit(solution)/shard_map/ppermute | solution.py:18
  151.5 74.3 %copy-start.27 = (f32[768]{0:T(1024)}, f32[768]{0:T(1024)S(1)}, u32[]{:S(2)}) copy-start(f32[768]{0:T(1024)S(1)} %convert_element_type.183) | copy-start | bytes 9220
  186.9 15.7 %collective-permute-start.6 = (bf16[384,768]{1,0:T(8,128)(2,1)}, bf16[384,768]{1,0:T(8,128)(2,1)S(1)}, u32[]{:S(2)}, u32[]{:S(2)}) collective-permute-start(bf16[384,768]{1,0:T(8,128)(2,1)} %collective-permute-done.5), channel_id=1, source_target_pairs={{0,7},{1,0},{2,1},{3,2},{4,3},{5,4},{6,5},{7,6},{8,15},{9,8},{10,9... | collective-permute-start | bytes 1769480 | tf_op jit(solution)/shard_map/ppermute | solution.py:20
  215.8 111.3 %all-to-all-start.3 = ((bf16[8,128,768]{2,1,0:T(8,128)(2,1)}), bf16[8,128,768]{2,1,0:T(8,128)(2,1)}, u32[]{:S(2)}, u32[]{:S(2)}) async-start(bf16[8,128,768]{2,1,0:T(8,128)(2,1)} %bitcast.183), calls=%async_computation.3 | async-start | bytes 3145728 | tf_op jit(solution)/shard_map/all_to_all | solution.py:206
  222.2 301.7 %reduce-scatter.7.cloned.1.call-start = ((), (), s32[]{:S(2)}) async-start(), calls=%async_computation.13 | async-start | bytes 1327104 | tf_op jit(solution)/shard_map/reduce_scatter | solution.py:292
  369.2 183.4 %reduce-scatter.5.cloned.1.call-start = ((), (), s32[]{:S(2)}) async-start(), calls=%async_computation.12 | async-start | bytes 3981312 | tf_op jit(solution)/shard_map/reduce_scatter | solution.py:289
  392.1 262.8 %reduce-scatter.9.cloned.1.call-start = ((), (), s32[]{:S(2)}) async-start(), calls=%async_computation.14 | async-start | bytes 5308416 | tf_op jit(solution)/shard_map/reduce_scatter | solution.py:301
  402.9 350.9 %reduce-scatter.11.cloned.1.call-start = ((), (), s32[]{:S(2)}) async-start(), calls=%async_computation.15 | async-start | bytes 5308416 | tf_op jit(solution)/shard_map/reduce_scatter | solution.py:307
  424.7 94.7 %all-to-all-start.4 = ((bf16[8,128,768]{2,1,0:T(8,128)(2,1)}), bf16[8,128,768]{2,1,0:T(8,128)(2,1)S(1)}, u32[]{:S(2)}, u32[]{:S(2)}) async-start(bf16[8,128,768]{2,1,0:T(8,128)(2,1)} %bitcast.172), calls=%async_computation.4 | async-start | bytes 3145728 | tf_op jit(solution)/shard_map/all_to_all | solution.py:280
  519.4 235.7 %copy-start.36 = (s32[128]{0:T(128)S(1)}, s32[128]{0:T(128)}, u32[]{:S(2)}) copy-start(s32[128]{0:T(128)} %copy-done.35) | copy-start | bytes 1540
  519.4 246.9 %copy-start.8 = (bf16[1024,768]{1,0:T(8,128)(2,1)S(1)}, bf16[1024,768]{1,0:T(8,128)(2,1)}, u32[]{:S(2)}) copy-start(bf16[1024,768]{1,0:T(8,128)(2,1)} %add_convert_fusion) | copy-start | bytes 4718596
  519.4 250.5 %all-to-all-start.2 = ((bf16[8,128,768]{2,1,0:T(8,128)(2,1)}), bf16[8,128,768]{2,1,0:T(8,128)(2,1)}, u32[]{:S(2)}, u32[]{:S(2)}) async-start(bf16[8,128,768]{2,1,0:T(8,128)(2,1)} %bitcast.191), calls=%async_computation.2 | async-start | bytes 3145728 | tf_op jit(solution)/shard_map/all_to_all | solution.py:201
  523.9 278.9 %all-reduce.17.cloned.1.call-start = ((), (), s32[]{:S(2)}) async-start(), calls=%async_computation.16 | async-start | bytes 3538944 | tf_op jit(solution)/shard_map/psum | solution.py:317
  (42 other events, 547.4 us)
Sparse Core Ops, SparseCore 0:
  10.2 115.4 all-gather.4
  127.9 56.7 all-gather.6
  186.9 102.8 all-gather.8
  369.3 64.1 reduce-scatter.6
  437.0 115.5 reduce-scatter.4
  556.1 98.7 reduce-scatter.8
  658.6 95.1 reduce-scatter.10
  756.4 46.3 all-reduce.16
